TPU v7x, 128 devices: a whole 4x4x4 slice. The times are simulated.
128 devices in a mesh: dp: 16 (over y, z), mp: 8 (over x, core).
Axes of the slice: x: 4, y: 4, z: 4, core: 2. Of those that a mesh axis runs over, the one named last changes fastest.
Arguments:
- hidden_in: bfloat16 [4096, 2304], P('dp'), may hold values from -6 to 6
- attn_gain: float32 [2304], replicated, may hold values from 0.25 to 1.75
- w_query: bfloat16 [2304, 2048], P(None, 'mp'), may hold values from -0.25 to 0.25
- w_key: bfloat16 [2304, 2048], P(None, 'mp'), may hold values from -0.125 to 0.125
- w_value: bfloat16 [2304, 2048], P(None, 'mp'), may hold values from -0.125 to 0.125
- w_out: bfloat16 [2048, 2304], P('mp'), may hold values from -0.5 to 0.5
- root_cache: bfloat16 [2, 4096, 2048], P(None, 'dp', 'mp'), may hold values from -400 to 400
- mid_cache: bfloat16 [2, 16, 1024, 2048], P(None, 'dp', None, 'mp'), may hold values from -400 to 400
- leaf_cache: bfloat16 [2, 32, 1024, 2048], P(None, 'dp', None, 'mp'), may hold values from -400 to 400
- mid_len: int32 [16], P('dp'), may hold values from 1 to 1024, 8192 in all
- leaf_len: int32 [32], P('dp'), may hold values from 1 to 1024, 16384 in all
- leaf_of: int32 [128], P('dp'), may hold values from 0 to 31, as said below
- parents: int32 [32], replicated, may hold values from 0 to 15, as said below
- suffix_len: int32 [128], P('dp'), may hold values from 1 to 32, 3072 in all
- ffn_gain: float32 [2304], replicated, may hold values from 0.25 to 1.75
- w_router: float32 [2304, 8], replicated, may hold values from -0.5 to 0.5
- routes: int32 [4096, 2], P('dp'), may hold values from 0 to 7, all different within a row; in each aligned block of 256 rows (0 to 255, 256 to 511, ...) at most 96 rows name the same one
- w_gate: bfloat16 [8, 2304, 5760], P('mp', None, 'dp'), may hold values from -0.125 to 0.125
- w_up: bfloat16 [8, 2304, 5760], P('mp', None, 'dp'), may hold values from -0.125 to 0.125
- w_down: bfloat16 [8, 5760, 2304], P('mp', 'dp'), may hold values from -0.078125 to 0.078125
Outputs:
- layer_out: bfloat16 [4096, 2304], P(('dp', 'mp'))
Inputs may be any that keep to these rules, and one draw needn't show every extreme that they name: `leaf_of`: leaf n belongs to index n // 2 of dp, mid-level node n to index n. The 8 sequences of one index of dp have different mid-level nodes and leaves of one parity, so that no two of them share a mid-level node or a leaf's owner. `parents`: every mid-level node is the parent of exactly one even and one odd leaf. `routes`: in the rows of one index of dp no expert is named by more than 96 rows; some indices of dp reach 96.
All inputs are finite; a program needn't handle non-finite values. No bound on the sum of `mid_len` or of `leaf_len` or of `suffix_len` on one device may be relied on, other than what follows from the above.
Results may differ from a plain program's by a relative error of at most 0.015.
The roundings to bfloat16 on the way count: a program that leaves them out, or rounds other values in their place, can miss the bound.
Values may be sent and summed in bfloat16 or wider, within the bound.
A program may use at most 128 MiB of HBM per device.

v0:
```python
import math
import jax
import jax.numpy as jnp
from jax import lax
from jax.sharding import PartitionSpec as P

HD = 64
TOP = 2
EPS = 1e-05
NEGATIVE = -1e30


def rms_scale(rows, gain):
    rows_wide = rows.astype(jnp.float32)
    mean_square = jnp.mean(rows_wide * rows_wide, axis=-1, keepdims=True)
    return rows_wide * lax.rsqrt(mean_square + EPS) * gain


def level_partial(queries, node_keys, node_values, limits, heads_here, batched):
    senders, row_count, width = queries.shape
    head_dim = width // heads_here
    scale = 1.0 / math.sqrt(head_dim)
    query_heads = queries.reshape(senders, row_count, heads_here, head_dim)
    if batched:
        key_heads = node_keys.reshape(senders, -1, heads_here, head_dim)
        value_heads = node_values.reshape(senders, -1, heads_here, head_dim)
        scores = jnp.einsum(
            "sqhd,skhd->sqhk", query_heads, key_heads, preferred_element_type=jnp.float32
        )
    else:
        key_heads = node_keys.reshape(-1, heads_here, head_dim)
        value_heads = node_values.reshape(-1, heads_here, head_dim)
        scores = jnp.einsum(
            "sqhd,khd->sqhk", query_heads, key_heads, preferred_element_type=jnp.float32
        )
    scores = scores * scale
    slots = jnp.arange(scores.shape[-1], dtype=jnp.int32)
    allowed = slots[None, :] < limits[:, None]
    scores = jnp.where(allowed[:, None, None, :], scores, NEGATIVE)
    peak = jnp.max(scores, axis=-1)
    weights = jnp.exp(scores - peak[..., None])
    total = jnp.sum(weights, axis=-1)
    probs = weights.astype(jnp.bfloat16)
    if batched:
        summed = jnp.einsum(
            "sqhk,skhd->sqhd", probs, value_heads, preferred_element_type=jnp.float32
        )
    else:
        summed = jnp.einsum(
            "sqhk,khd->sqhd", probs, value_heads, preferred_element_type=jnp.float32
        )
    result = (summed / total[..., None]).reshape(senders, row_count, width)
    return (result, peak + jnp.log(total))


def on_device(
    hidden_in,
    attn_gain,
    w_query,
    w_key,
    w_value,
    w_out,
    root_cache,
    mid_cache,
    leaf_cache,
    mid_len,
    leaf_len,
    leaf_of,
    parents,
    suffix_len,
    ffn_gain,
    w_router,
    routes,
    w_gate,
    w_up,
    w_down,
):
    tok_rows, width = hidden_in.shape
    seq_rows = suffix_len.shape[0]
    suffix = tok_rows // seq_rows
    head_dim = HD
    local_width = w_query.shape[1]
    heads_here = local_width // head_dim
    scale = 1.0 / math.sqrt(head_dim)
    owners = lax.axis_size("dp")
    normed = rms_scale(hidden_in, attn_gain).astype(jnp.bfloat16)
    query = jnp.dot(normed, w_query, preferred_element_type=jnp.float32).astype(jnp.bfloat16)
    key = jnp.dot(normed, w_key, preferred_element_type=jnp.float32).astype(jnp.bfloat16)
    value = jnp.dot(normed, w_value, preferred_element_type=jnp.float32).astype(jnp.bfloat16)
    query_heads = query.reshape(tok_rows, heads_here, head_dim)
    piece = lax.all_gather(root_cache, "dp", axis=1, tiled=True)
    running_peak = jnp.full((tok_rows, heads_here), NEGATIVE, jnp.float32)
    piece_keys = piece[0].reshape(-1, heads_here, head_dim)
    piece_values = piece[1].reshape(-1, heads_here, head_dim)
    scores = (
        jnp.einsum("qhd,khd->qhk", query_heads, piece_keys, preferred_element_type=jnp.float32)
        * scale
    )
    new_peak = jnp.maximum(running_peak, jnp.max(scores, axis=-1))
    weights = jnp.exp(scores - new_peak[..., None])
    new_total = jnp.sum(weights, axis=-1)
    added = jnp.einsum(
        "qhk,khd->qhd",
        weights.astype(jnp.bfloat16),
        piece_values,
        preferred_element_type=jnp.float32,
    )
    root_out = added / new_total[..., None]
    root_lse = new_peak + jnp.log(new_total)
    query_seq = query.reshape(seq_rows, suffix, heads_here, head_dim)
    key_seq = key.reshape(seq_rows, suffix, heads_here, head_dim)
    value_seq = value.reshape(seq_rows, suffix, heads_here, head_dim)
    slots = jnp.arange(suffix, dtype=jnp.int32)
    self_ok = (slots[None, None, :] <= slots[None, :, None]) & (
        slots[None, None, :] < suffix_len[:, None, None]
    )
    self_scores = (
        jnp.einsum("sqhd,skhd->sqhk", query_seq, key_seq, preferred_element_type=jnp.float32)
        * scale
    )
    self_scores = jnp.where(self_ok[:, :, None, :], self_scores, NEGATIVE)
    self_peak = jnp.max(self_scores, axis=-1)
    self_weights = jnp.exp(self_scores - self_peak[..., None])
    self_total = jnp.sum(self_weights, axis=-1)
    self_sum = jnp.einsum(
        "sqhk,skhd->sqhd",
        self_weights.astype(jnp.bfloat16),
        value_seq,
        preferred_element_type=jnp.float32,
    )
    self_out = (self_sum / self_total[..., None]).reshape(tok_rows, heads_here, head_dim)
    self_lse = (self_peak + jnp.log(self_total)).reshape(tok_rows, heads_here)
    mid_of = parents[leaf_of]
    leaf_owner = leaf_of // 2
    leaf_side = (leaf_of % 2).astype(jnp.float32)
    targets = jnp.arange(owners, dtype=jnp.int32)
    pick_mid = (mid_of[None, :] == targets[:, None]).astype(jnp.bfloat16)
    pick_leaf = (leaf_owner[None, :] == targets[:, None]).astype(jnp.bfloat16)
    flat_query = query.reshape(seq_rows, suffix * local_width)
    sent_mid = jnp.dot(pick_mid, flat_query, preferred_element_type=jnp.float32).astype(
        jnp.bfloat16
    )
    sent_leaf = jnp.dot(pick_leaf, flat_query, preferred_element_type=jnp.float32).astype(
        jnp.bfloat16
    )
    sent = jnp.stack([sent_mid, sent_leaf], axis=1).reshape(owners, 2, suffix, local_width)
    side_of_target = jnp.dot(
        pick_leaf.astype(jnp.float32), leaf_side, precision=lax.Precision.HIGHEST
    )
    sides = jnp.stack([jnp.zeros_like(side_of_target), side_of_target], axis=1)
    sides = jnp.broadcast_to(sides[:, :, None], (owners, 2, suffix)).astype(jnp.bfloat16)
    sent_queries = lax.all_to_all(sent, "dp", split_axis=0, concat_axis=0, tiled=True)
    sent_sides = lax.all_to_all(sides, "dp", split_axis=0, concat_axis=0, tiled=True)
    senders = sent_queries.shape[0]
    second = sent_sides[:, 1, 0] > 0.5
    mid_limit = jnp.broadcast_to(mid_len[0], (senders,))
    mid_result, mid_logsum = level_partial(
        sent_queries[:, 0], mid_cache[0, 0], mid_cache[1, 0], mid_limit, heads_here, False
    )
    leaf_keys = jnp.where(second[:, None, None], leaf_cache[0, 1][None], leaf_cache[0, 0][None])
    leaf_values = jnp.where(second[:, None, None], leaf_cache[1, 1][None], leaf_cache[1, 0][None])
    leaf_limit = jnp.where(second, leaf_len[1], leaf_len[0])
    leaf_result, leaf_logsum = level_partial(
        sent_queries[:, 1], leaf_keys, leaf_values, leaf_limit, heads_here, True
    )
    owner_out = jnp.stack([mid_result, leaf_result], axis=1)
    owner_lse = jnp.stack([mid_logsum, leaf_logsum], axis=1)
    back_out, back_lse = (
        lax.all_to_all(owner_out, "dp", split_axis=0, concat_axis=0, tiled=True),
        lax.all_to_all(owner_lse, "dp", split_axis=0, concat_axis=0, tiled=True),
    )
    mid_out = back_out[mid_of, 0].reshape(tok_rows, heads_here, head_dim)
    mid_lse = back_lse[mid_of, 0].reshape(tok_rows, heads_here)
    leaf_out = back_out[leaf_owner, 1].reshape(tok_rows, heads_here, head_dim)
    leaf_lse = back_lse[leaf_owner, 1].reshape(tok_rows, heads_here)
    stacked_lse = jnp.stack([root_lse, mid_lse, leaf_lse, self_lse])
    stacked_out = jnp.stack([root_out, mid_out, leaf_out, self_out])
    overall = jnp.max(stacked_lse, axis=0)
    shares = jnp.exp(stacked_lse - overall)
    combined = jnp.sum(shares[..., None] * stacked_out, axis=0) / jnp.sum(shares, axis=0)[..., None]
    attended = combined.reshape(tok_rows, local_width).astype(jnp.bfloat16)
    projected = jnp.dot(attended, w_out, preferred_element_type=jnp.float32)
    rows_here = tok_rows // lax.axis_size("mp")
    first = lax.axis_index("mp") * rows_here
    attn_all = lax.psum(projected, "mp")
    resid_all = hidden_in.astype(jnp.float32) + attn_all
    ffn_in = rms_scale(resid_all, ffn_gain).astype(jnp.bfloat16)
    resid = lax.dynamic_slice_in_dim(resid_all, first, rows_here, 0)
    logits = jnp.dot(ffn_in.astype(jnp.float32), w_router, precision=lax.Precision.HIGHEST)
    chosen = jnp.take_along_axis(logits, routes, axis=1)
    squashed = jax.nn.sigmoid(chosen)
    gates = squashed / jnp.sum(squashed, axis=1, keepdims=True)
    expert = lax.axis_index("mp")
    hit_each = routes == expert
    hit = jnp.any(hit_each, axis=1)
    gate_here = jnp.sum(jnp.where(hit_each, gates, 0.0), axis=1)
    order = jnp.cumsum(hit.astype(jnp.int32)) - 1
    capacity = 3 * TOP * tok_rows // (2 * lax.axis_size("mp"))
    slot_ids = jnp.arange(capacity, dtype=jnp.int32)
    pick_slot = (order[None, :] == slot_ids[:, None]) & hit[None, :]
    dispatch = jnp.dot(
        pick_slot.astype(jnp.bfloat16), ffn_in, preferred_element_type=jnp.float32
    ).astype(jnp.bfloat16)
    slot_gate = jnp.dot(pick_slot.astype(jnp.float32), gate_here, precision=lax.Precision.HIGHEST)
    gate_weight = w_gate[0]
    up_weight = w_up[0]
    down_weight = w_down[0]
    piece = lax.all_gather(dispatch, "dp", axis=0, tiled=True)
    gate_part = jnp.dot(piece, gate_weight, preferred_element_type=jnp.float32)
    up_part = jnp.dot(piece, up_weight, preferred_element_type=jnp.float32)
    partial_out = jnp.dot(
        (jax.nn.silu(gate_part) * up_part).astype(jnp.bfloat16),
        down_weight,
        preferred_element_type=jnp.float32,
    )
    expert_out = lax.psum_scatter(partial_out, "dp", scatter_dimension=0, tiled=True)
    weighted = expert_out * slot_gate[:, None]
    spread = jnp.dot(pick_slot.astype(jnp.float32).T, weighted, precision=lax.Precision.HIGHEST)
    mixed = lax.psum_scatter(spread, "mp", scatter_dimension=0, tiled=True)
    row_ids = first + jnp.arange(rows_here, dtype=jnp.int32)
    valid = row_ids % suffix < suffix_len[row_ids // suffix]
    return jnp.where(valid[:, None], resid + mixed, 0.0).astype(jnp.bfloat16)


def solution(mesh):
    return jax.shard_map(
        on_device,
        mesh=mesh,
        in_specs=(
            P("dp", None),
            P(),
            P(None, "mp"),
            P(None, "mp"),
            P(None, "mp"),
            P("mp", None),
            P(None, "dp", "mp"),
            P(None, "dp", None, "mp"),
            P(None, "dp", None, "mp"),
            P("dp"),
            P("dp"),
            P("dp"),
            P(),
            P("dp"),
            P(),
            P(),
            P("dp", None),
            P("mp", None, "dp"),
            P("mp", None, "dp"),
            P("mp", "dp", None),
        ),
        out_specs=P(("dp", "mp"), None),
        check_vma=False,
    )
```

profile of v0, /device:TPU:0, one launch (start us, length us, event | category | flops | bytes accessed | tf_op | source)
XLA Modules:
  0.0 482.1 jit_solution(8950069300431746591)
XLA Ops:
  9.6 8.1 %all-to-all-start.1 = ((bf16[16,2,32]{2,1,0:T(2,128)(2,1)}), bf16[16,2,32]{2,1,0:T(2,128)(2,1)S(1)}, u32[]{:S(2)}, u32[]{:S(2)}) async-start(bf16[16,2,32]{2,1,0:T(2,128)(2,1)} %broadcast_in_dim.168), calls=%async_computation.1 | async-start | bytes 16384 | tf_op jit(solution)/shard_map/all_to_all | solution.py:153
  34.5 7.6 %all-to-all-start = ((bf16[16,2,32,256]{3,2,1,0:T(8,128)(2,1)}), bf16[16,2,32,256]{3,2,1,0:T(8,128)(2,1)}, u32[]{:S(2)}, u32[]{:S(2)}) async-start(bf16[16,2,32,256]{3,2,1,0:T(8,128)(2,1)} %pad_maximum_fusion.1), calls=%async_computation | async-start | bytes 1048576 | tf_op jit(solution)/shard_map/all_to_all | solution.py:152
  62.5 4.5 bitcast_reduce_fusion.1
  69.3 2.7 fusion.64
  84.2 4.5 fusion.69
  93.0 7.1 %all-to-all-start.2 = ((f32[16,1,256]{2,1,0:T(1,128)}), f32[16,1,256]{2,1,0:T(1,128)S(1)}, u32[]{:S(2)}, u32[]{:S(2)}) async-start(f32[16,1,256]{2,1,0:T(1,128)} %reshape.482), calls=%async_computation.2 | async-start | bytes 32768 | tf_op jit(solution)/shard_map/all_to_all | solution.py:170
  102.3 5.3 %all-to-all-done.2 = f32[16,1,256]{2,1,0:T(1,128)S(1)} async-done(((f32[16,1,256]{2,1,0:T(1,128)}), f32[16,1,256]{2,1,0:T(1,128)S(1)}, u32[]{:S(2)}, u32[]{:S(2)}) %all-to-all-start.2) | async-done | bytes 16416 | tf_op jit(solution)/shard_map/all_to_all | solution.py:170
  107.7 4.3 all-to-all-start.3
  123.5 3.6 all-to-all-done.3
  136.3 4.5 fusion.133
  140.7 4.3 copy.247
  145.0 4.1 copy.269
  149.1 9.7 %bitcast_reduce_fusion = (f32[256,4]{0,1:T(4,128)S(1)}, f32[4,256,4096]{2,1,0:T(8,128)}) fusion(bf16[256,4,64]{0,2,1:T(8,128)(2,1)S(1)} %bitcast.204, bf16[4096,4,64]{0,2,1:T(8,128)(2,1)} %bitcast.186), kind=kOutput, calls=%fused_computation.8 | convolution fusion | flops 545258496 | bytes 19009536 | tf_op jit(solution)/shard_map/qhd,khd->qhk/dot_general | solution.py:96
  158.8 8.6 %fusion.2 = f32[256,4]{0,1:T(4,128)S(1)} fusion(f32[4,256,4096]{2,1,0:T(8,128)} %get-tuple-element.35, f32[256,4]{0,1:T(4,128)S(1)} %broadcast_maximum_fusion), kind=kLoop, calls=%fused_computation.11 | loop fusion | flops 12581888 | bytes 16785408 | tf_op jit(solution)/shard_map/reduce_sum | solution.py:101
  167.5 10.2 %fusion.60 = f32[1,256,4,64]{1,3,2,0:T(8,128)} fusion(bf16[4096,4,64]{0,2,1:T(8,128)(2,1)} %bitcast.188, f32[4,256,4096]{2,1,0:T(8,128)} %get-tuple-element.35, f32[256,4]{0,1:T(4,128)S(1)} %broadcast_maximum_fusion, f32[256,4]{0,1:T(4,128)S(1)} %fusion.2), kind=kOutput, calls=%fused_computation.76 | convolution fusion | flops 549519360 | bytes 19144704 | tf_op jit(solution)/shard_map/qhk,khd->qhd/dot_general | solution.py:102
  181.7 63.8 %all-reduce.5.cloned.1.call-done = f32[256,2304]{1,0:T(8,128)} async-done(((f32[256,2304]{1,0:T(8,128)}), f32[256,2304]{1,0:T(8,128)}) %all-reduce.5.cloned.1.call-update) | async-done | bytes 2359312 | tf_op jit(solution)/shard_map/psum | solution.py:185
  250.6 64.6 %all-gather.5.cloned.1.call-done = bf16[1536,2304]{1,0:T(8,128)(2,1)} async-done(((bf16[96,2304]{1,0:T(8,128)(2,1)}), bf16[1536,2304]{1,0:T(8,128)(2,1)}) %all-gather.5.cloned.1.call-update) | async-done | bytes 7077904 | tf_op jit(solution)/shard_map/all_gather | solution.py:208
  315.2 7.7 %fusion.36 = f32[1536,360]{0,1:T(8,128)} fusion(bf16[1536,2304]{1,0:T(8,128)(2,1)} %all-gather.5.cloned.1.call-done, bf16[1,2304,360]{1,2,0:T(8,128)(2,1)} %param.37), kind=kOutput, calls=%fused_computation.57 | convolution fusion | flops 2548039680 | bytes 10948608 | tf_op jit(solution)/shard_map/dot_general | solution.py:209
  322.8 14.3 %fusion.33 = f32[1536,2304]{1,0:T(8,128)} fusion(bf16[1,360,2304]{2,1,0:T(8,128)(2,1)S(1)} %copy-done, bf16[1536,2304]{1,0:T(8,128)(2,1)} %all-gather.5.cloned.1.call-done, f32[1536,360]{0,1:T(8,128)} %fusion.36, bf16[1,2304,360]{1,2,0:T(8,128)(2,1)} %param.38), kind=kOutput, calls=%fused_computation.54 | convolution fusion | flops 5099397120 | bytes 26763264 | tf_op jit(solution)/shard_map/dot_general | solution.py:211
  338.0 2.7 fusion.127
  340.7 3.6 gather_fusion.6
  344.7 92.1 %reduce-scatter.3.cloned.1.call-done = f32[96,2304]{1,0:T(8,128)} async-done(((f32[1536,2304]{1,0:T(8,128)}), f32[96,2304]{1,0:T(8,128)}) %reduce-scatter.3.cloned.1.call-update) | async-done | bytes 884752 | tf_op jit(solution)/shard_map/reduce_scatter | solution.py:216
  436.8 3.9 fusion.72
  441.4 32.1 %reduce-scatter.5.cloned.1.call-done = f32[32,2304]{1,0:T(8,128)} async-done(((f32[256,2304]{1,0:T(8,128)}), f32[32,2304]{1,0:T(8,128)}) %reduce-scatter.5.cloned.1.call-update) | async-done | bytes 294928 | tf_op jit(solution)/shard_map/reduce_scatter | solution.py:219
  (199 shorter events, 93.7 us)
Async XLA Ops:
  6.5 316.3 %copy-start = (bf16[1,360,2304]{2,1,0:T(8,128)(2,1)S(1)}, bf16[1,360,2304]{2,1,0:T(8,128)(2,1)}, u32[]{:S(2)}) copy-start(bf16[1,360,2304]{2,1,0:T(8,128)(2,1)} %param.39) | copy-start | bytes 4976644
  6.5 129.7 %all-gather.3.cloned.1.call-start = ((), (), s32[]{:S(2)}) async-start(), calls=%async_computation.6 | async-start | bytes 4456448 | tf_op jit(solution)/shard_map/all_gather | solution.py:91
  9.6 24.9 %all-to-all-start.1 = ((bf16[16,2,32]{2,1,0:T(2,128)(2,1)}), bf16[16,2,32]{2,1,0:T(2,128)(2,1)S(1)}, u32[]{:S(2)}, u32[]{:S(2)}) async-start(bf16[16,2,32]{2,1,0:T(2,128)(2,1)} %broadcast_in_dim.168), calls=%async_computation.1 | async-start | bytes 16384 | tf_op jit(solution)/shard_map/all_to_all | solution.py:153
  19.4 5.5 %copy-start.35 = (f32[256]{0:T(256)}, f32[256]{0:T(256)S(1)}, u32[]{:S(2)}) copy-start(f32[256]{0:T(256)S(1)} %add_rsqrt_fusion.1) | copy-start | bytes 3076
  26.9 4.9 %copy-start.7 = (bf16[2,2,1024,256]{3,2,1,0:T(8,128)(2,1)S(1)}, bf16[2,2,1024,256]{3,2,1,0:T(8,128)(2,1)}, u32[]{:S(2)}) copy-start(bf16[2,2,1024,256]{3,2,1,0:T(8,128)(2,1)} %param.28) | copy-start | bytes 6291460
  34.5 22.1 %all-to-all-start = ((bf16[16,2,32,256]{3,2,1,0:T(8,128)(2,1)}), bf16[16,2,32,256]{3,2,1,0:T(8,128)(2,1)}, u32[]{:S(2)}, u32[]{:S(2)}) async-start(bf16[16,2,32,256]{3,2,1,0:T(8,128)(2,1)} %pad_maximum_fusion.1), calls=%async_computation | async-start | bytes 1048576 | tf_op jit(solution)/shard_map/all_to_all | solution.py:152
  78.7 5.5 %copy-start.15 = (bf16[1,1,1024,256]{2,3,1,0:T(8,128)(2,1)S(1)}, bf16[1,1,1024,256]{2,3,1,0:T(8,128)(2,1)}, u32[]{:S(2)}) copy-start(bf16[1,1,1024,256]{2,3,1,0:T(8,128)(2,1)} %copy.270) | copy-start | bytes 1572868
  88.7 11.4 %copy-start.8 = (f32[16,1,32,256]{3,2,0,1:T(8,128)S(1)}, f32[16,1,32,256]{3,2,0,1:T(8,128)}, u32[]{:S(2)}) copy-start(f32[16,1,32,256]{3,2,0,1:T(8,128)} %stack_reshape.25) | copy-start | bytes 1572868
  93.0 19.1 %copy-start.25 = (f32[8,32,4]{1,2,0:T(4,128)S(1)}, f32[8,32,4]{1,2,0:T(4,128)}, u32[]{:S(2)}) copy-start(f32[8,32,4]{1,2,0:T(4,128)} %copy-done.24) | copy-start | bytes 12292
  93.0 19.1 %copy-start.26 = (f32[8,32,4]{1,2,0:T(4,128)S(1)}, f32[8,32,4]{1,2,0:T(4,128)}, u32[]{:S(2)}) copy-start(f32[8,32,4]{1,2,0:T(4,128)} %fusion.78) | copy-start | bytes 12292
  93.0 20.4 %copy-start.36 = (f32[256]{0:T(256)S(1)}, f32[256]{0:T(256)}, u32[]{:S(2)}) copy-start(f32[256]{0:T(256)} %copy-done.35) | copy-start | bytes 3076
  93.0 14.6 %all-to-all-start.2 = ((f32[16,1,256]{2,1,0:T(1,128)}), f32[16,1,256]{2,1,0:T(1,128)S(1)}, u32[]{:S(2)}, u32[]{:S(2)}) async-start(f32[16,1,256]{2,1,0:T(1,128)} %reshape.482), calls=%async_computation.2 | async-start | bytes 32768 | tf_op jit(solution)/shard_map/all_to_all | solution.py:170
  107.7 19.4 %all-to-all-start.3 = ((f32[16,2,32,256]{3,2,1,0:T(8,128)}), f32[16,2,32,256]{3,2,1,0:T(8,128)}, u32[]{:S(2)}, u32[]{:S(2)}) async-start(f32[16,2,32,256]{3,2,1,0:T(8,128)} %pad_maximum_fusion), calls=%async_computation.3 | async-start | bytes 2097152 | tf_op jit(solution)/shard_map/all_to_all | solution.py:169
  112.0 5.7 %copy-start.14 = (f32[8,32,4,32]{1,3,2,0:T(8,128)S(1)}, f32[8,32,4,32]{1,3,2,0:T(8,128)}, u32[]{:S(2)}) copy-start(f32[8,32,4,32]{1,3,2,0:T(8,128)} %copy-done.13) | copy-start | bytes 393220
  112.1 133.5 %all-reduce.5.cloned.1.call-start = ((), (), s32[]{:S(2)}) async-start(), calls=%async_computation.7 | async-start | bytes 4718592 | tf_op jit(solution)/shard_map/psum | solution.py:185
  167.4 10.2 %copy-start.31 = (f32[256,4]{0,1:T(4,128)S(1)}, f32[256,4]{0,1:T(4,128)}, u32[]{:S(2)}) copy-start(f32[256,4]{0,1:T(4,128)} %add.217) | copy-start | bytes 12292
  167.4 10.2 %copy-start.30 = (f32[1,256,4]{1,2,0:T(4,128)S(1)}, f32[1,256,4]{1,2,0:T(4,128)}, u32[]{:S(2)}) copy-start(f32[1,256,4]{1,2,0:T(4,128)} %add.216) | copy-start | bytes 12292
  167.4 10.3 %copy-start.11 = (f32[1,256,4,64]{1,3,2,0:T(8,128)S(1)}, f32[1,256,4,64]{1,3,2,0:T(8,128)}, u32[]{:S(2)}) copy-start(f32[1,256,4,64]{1,3,2,0:T(8,128)} %copy.282) | copy-start | bytes 786436
  167.4 10.3 %copy-start.12 = (f32[1,256,4,64]{1,3,2,0:T(8,128)S(1)}, f32[1,256,4,64]{1,3,2,0:T(8,128)}, u32[]{:S(2)}) copy-start(f32[1,256,4,64]{1,3,2,0:T(8,128)} %copy.281) | copy-start | bytes 786436
  181.0 134.1 %all-gather.5.cloned.1.call-start = ((), (), s32[]{:S(2)}) async-start(), calls=%async_computation.8 | async-start | bytes 7520256 | tf_op jit(solution)/shard_map/all_gather | solution.py:208
  181.7 67.4 %copy-start.28 = (f32[2304]{0:T(1024)S(1)}, f32[2304]{0:T(1024)}, u32[]{:S(2)}) copy-start(f32[2304]{0:T(1024)} %param.34) | copy-start | bytes 27652
  250.3 186.5 %reduce-scatter.3.cloned.1.call-start = ((), (), s32[]{:S(2)}) async-start(), calls=%async_computation.9 | async-start | bytes 15040512 | tf_op jit(solution)/shard_map/reduce_scatter | solution.py:216
  337.1 136.4 %reduce-scatter.5.cloned.1.call-start = ((), (), s32[]{:S(2)}) async-start(), calls=%async_computation.10 | async-start | bytes 2654208 | tf_op jit(solution)/shard_map/reduce_scatter | solution.py:219
  436.8 38.6 %copy-start.1 = (bf16[1,360,2304]{2,1,0:T(8,128)(2,1)S(1)}, bf16[1,360,2304]{2,1,0:T(8,128)(2,1)}, u32[]{:S(2)}) copy-start(bf16[1,360,2304]{2,1,0:T(8,128)(2,1)} %param.39) | copy-start | bytes 4976644
  (24 other events, 61.4 us)
Sparse Core Ops, SparseCore 0:
  9.6 59.1 all-gather.2
  181.1 64.3 all-reduce.4
  250.4 64.6 all-gather.4
  337.3 99.4 reduce-scatter.2
  440.8 32.7 reduce-scatter.4
where the time goes:
time: 487 us; the launch traced here: 482 us
  waiting for transfers between devices  263 us (54%)
  matrix products  76.3 us (16%)
  local copies, waits for them, and re-layouts  71.5 us (15%)
  other arithmetic  29.4 us (6%)
  starting transfers between devices  27.5 us (6%)
  between operations  14.7 us (3%)
    reduce_scatter x1, waiting for transfers between devices, on_device(): lax.psum_scatter(partial_out, 'dp', scatter_dimension=0, tiled=True)  92.1 us
    all_gather x1, waiting for transfers between devices, on_device(): piece = lax.all_gather(dispatch, 'dp', axis=0, tiled=True)  64.6 us
    psum x1, waiting for transfers between devices, on_device(): attn_all = lax.psum(projected, 'mp')  63.8 us
    reduce_scatter x1, waiting for transfers between devices, on_device(): mixed = lax.psum_scatter(spread, 'mp', scatter_dimension=0, tiled=True)  32.1 us
    dot_general x1, matrix products, on_device(): jnp.dot((jax.nn.silu(gate_part) * up_part).astype(jnp.bfloat16), down_wei...  14.3 us
    unnamed x87, local copies, waits for them, and re-layouts  13.6 us
    dot_general x1, matrix products, on_device(): jnp.einsum('qhk,khd->qhd', weights.astype(jnp.bfloat16), piece_values, pr...  10.2 us
  transfers between devices with their start and end apart: 9, of which 7 were waited for; matrix products, arithmetic and copies ran while one was open for 20% of the time, Pallas kernels for 0%

commit v1 on v0

--- a/solution.py
+++ b/solution.py
@@ -205,7 +205,9 @@
     gate_weight = w_gate[0]
     up_weight = w_up[0]
     down_weight = w_down[0]
-    piece = lax.all_gather(dispatch, "dp", axis=0, tiled=True)
+    piece = jnp.concatenate(
+        lax.all_to_all(jnp.stack([dispatch] * lax.axis_size("dp")), "dp", 0, 0), axis=0
+    )
     gate_part = jnp.dot(piece, gate_weight, preferred_element_type=jnp.float32)
     up_part = jnp.dot(piece, up_weight, preferred_element_type=jnp.float32)
     partial_out = jnp.dot(

time: 487 us -> 508 us (1.043)
  blocking collectives: 0 us -> 86.7 us
  waiting for transfers between devices: 263 us -> 197 us
    all_to_all x0 -> x1, blocking collectives: none -> 86.7 us  [on_device(): lax.all_to_all(jnp.stack([dispatch] * lax.axis_size('dp')), 'dp', 0, 0)]
    all_gather x1 -> x0, waiting for transfers between devices: 64.6 us -> none  [on_device(): piece = lax.all_gather(dispatch, 'dp', axis=0, tiled=True)]
    unnamed x87 -> x91, local copies, waits for them, and re-layouts: 13.6 us -> 16.4 us
  transfers between devices with their start and end apart: 9 -> 8, of which waited for: 7 -> 6; matrix products, arithmetic and copies ran while one was open for 20% -> 20% of each run, Pallas kernels for 0% -> 0%
where the time goes in v1:
time: 508 us; the launch traced here: 503 us
  waiting for transfers between devices  197 us (39%)
  blocking collectives  86.7 us (17%)
  local copies, waits for them, and re-layouts  75 us (15%)
  matrix products  72.1 us (14%)
  other arithmetic  29.5 us (6%)
  starting transfers between devices  27.5 us (5%)
  between operations  14.7 us (3%)
    reduce_scatter x1, waiting for transfers between devices, on_device(): lax.psum_scatter(partial_out, 'dp', scatter_dimension=0, tiled=True)  91.2 us
    all_to_all x1, blocking collectives, on_device(): lax.all_to_all(jnp.stack([dispatch] * lax.axis_size('dp')), 'dp', 0, 0)  86.7 us
    psum x1, waiting for transfers between devices, on_device(): attn_all = lax.psum(projected, 'mp')  63.9 us
    reduce_scatter x1, waiting for transfers between devices, on_device(): mixed = lax.psum_scatter(spread, 'mp', scatter_dimension=0, tiled=True)  32.1 us
    unnamed x91, local copies, waits for them, and re-layouts  16.4 us
    dot_general x1, matrix products, on_device(): jnp.dot((jax.nn.silu(gate_part) * up_part).astype(jnp.bfloat16), down_wei...  14.3 us
    dot_general x1, matrix products, on_device(): jnp.einsum('qhk,khd->qhd', weights.astype(jnp.bfloat16), piece_values, pr...  10.2 us
  transfers between devices with their start and end apart: 8, of which 6 were waited for; matrix products, arithmetic and copies ran while one was open for 20% of the time, Pallas kernels for 0%

profile of v1, /device:TPU:0, one launch (start us, length us, event | category | flops | bytes accessed | tf_op | source)
XLA Modules:
  0.0 502.7 jit_solution(16222645508036659001)
XLA Ops:
  9.6 8.1 %all-to-all-start.1 = ((bf16[16,2,32]{2,1,0:T(2,128)(2,1)}), bf16[16,2,32]{2,1,0:T(2,128)(2,1)S(1)}, u32[]{:S(2)}, u32[]{:S(2)}) async-start(bf16[16,2,32]{2,1,0:T(2,128)(2,1)} %broadcast_in_dim.168), calls=%async_computation.1 | async-start | bytes 16384 | tf_op jit(solution)/shard_map/all_to_all | solution.py:153
  34.5 7.6 %all-to-all-start = ((bf16[16,2,32,256]{3,2,1,0:T(8,128)(2,1)}), bf16[16,2,32,256]{3,2,1,0:T(8,128)(2,1)}, u32[]{:S(2)}, u32[]{:S(2)}) async-start(bf16[16,2,32,256]{3,2,1,0:T(8,128)(2,1)} %pad_maximum_fusion.1), calls=%async_computation | async-start | bytes 1048576 | tf_op jit(solution)/shard_map/all_to_all | solution.py:152
  62.6 4.5 bitcast_reduce_fusion.1
  69.3 2.7 fusion.64
  84.2 4.5 fusion.69
  93.0 7.3 %all-to-all-start.2 = ((f32[16,1,256]{2,1,0:T(1,128)}), f32[16,1,256]{2,1,0:T(1,128)S(1)}, u32[]{:S(2)}, u32[]{:S(2)}) async-start(f32[16,1,256]{2,1,0:T(1,128)} %reshape.488), calls=%async_computation.2 | async-start | bytes 32768 | tf_op jit(solution)/shard_map/all_to_all | solution.py:170
  102.6 5.4 %all-to-all-done.2 = f32[16,1,256]{2,1,0:T(1,128)S(1)} async-done(((f32[16,1,256]{2,1,0:T(1,128)}), f32[16,1,256]{2,1,0:T(1,128)S(1)}, u32[]{:S(2)}, u32[]{:S(2)}) %all-to-all-start.2) | async-done | bytes 16416 | tf_op jit(solution)/shard_map/all_to_all | solution.py:170
  107.9 4.3 all-to-all-start.3
  123.8 3.5 all-to-all-done.3
  136.4 4.4 fusion.133
  140.8 4.3 copy.247
  145.1 4.1 copy.269
  149.2 9.7 %bitcast_reduce_fusion = (f32[256,4]{0,1:T(4,128)S(1)}, f32[4,256,4096]{2,1,0:T(8,128)}) fusion(bf16[256,4,64]{0,2,1:T(8,128)(2,1)S(1)} %bitcast.207, bf16[4096,4,64]{0,2,1:T(8,128)(2,1)} %bitcast.187), kind=kOutput, calls=%fused_computation.8 | convolution fusion | flops 545258496 | bytes 19009536 | tf_op jit(solution)/shard_map/qhd,khd->qhk/dot_general | solution.py:96
  158.9 8.6 %fusion.2 = f32[256,4]{0,1:T(4,128)S(1)} fusion(f32[4,256,4096]{2,1,0:T(8,128)} %get-tuple-element.35, f32[256,4]{0,1:T(4,128)S(1)} %broadcast_maximum_fusion), kind=kLoop, calls=%fused_computation.11 | loop fusion | flops 12581888 | bytes 16785408 | tf_op jit(solution)/shard_map/reduce_sum | solution.py:101
  167.6 10.2 %fusion.60 = f32[1,256,4,64]{1,3,2,0:T(8,128)} fusion(bf16[4096,4,64]{0,2,1:T(8,128)(2,1)} %bitcast.191, f32[4,256,4096]{2,1,0:T(8,128)} %get-tuple-element.35, f32[256,4]{0,1:T(4,128)S(1)} %broadcast_maximum_fusion, f32[256,4]{0,1:T(4,128)S(1)} %fusion.2), kind=kOutput, calls=%fused_computation.76 | convolution fusion | flops 549519360 | bytes 19144704 | tf_op jit(solution)/shard_map/qhk,khd->qhd/dot_general | solution.py:102
  181.8 63.9 %all-reduce.5.cloned.1.call-done = f32[256,2304]{1,0:T(8,128)} async-done(((f32[256,2304]{1,0:T(8,128)}), f32[256,2304]{1,0:T(8,128)}) %all-reduce.5.cloned.1.call-update) | async-done | bytes 2359312 | tf_op jit(solution)/shard_map/psum | solution.py:185
  250.5 86.7 %all_to_all.25 = bf16[16,96,2304]{2,1,0:T(8,128)(2,1)S(1)} all-to-all(bf16[16,96,2304]{2,1,0:T(8,128)(2,1)S(1)} %stack.69), channel_id=1, replica_groups=mesh['dp'=16,'mp'=8] {'dp'}, dimensions={0} | all-to-all | bytes 14155776 | tf_op jit(solution)/shard_map/all_to_all | solution.py:209
  337.2 2.8 copy-done.6
  340.0 4.2 fusion.36
  344.3 14.3 %fusion.33 = f32[1536,2304]{1,0:T(8,128)} fusion(bf16[1,360,2304]{2,1,0:T(8,128)(2,1)S(1)} %copy-done, bf16[1536,2304]{1,0:T(8,128)(2,1)} %bitcast.189, f32[1536,360]{0,1:T(8,128)} %fusion.36, bf16[1,2304,360]{1,2,0:T(8,128)(2,1)} %param.38), kind=kOutput, calls=%fused_computation.54 | convolution fusion | flops 5099397120 | bytes 26763264 | tf_op jit(solution)/shard_map/dot_general | solution.py:213
  362.2 3.6 gather_fusion.6
  366.1 91.2 %reduce-scatter.3.cloned.1.call-done = f32[96,2304]{1,0:T(8,128)} async-done(((f32[1536,2304]{1,0:T(8,128)}), f32[96,2304]{1,0:T(8,128)}) %reduce-scatter.3.cloned.1.call-update) | async-done | bytes 884752 | tf_op jit(solution)/shard_map/reduce_scatter | solution.py:218
  457.3 3.9 fusion.72
  462.0 32.1 %reduce-scatter.5.cloned.1.call-done = f32[32,2304]{1,0:T(8,128)} async-done(((f32[256,2304]{1,0:T(8,128)}), f32[32,2304]{1,0:T(8,128)}) %reduce-scatter.5.cloned.1.call-update) | async-done | bytes 294928 | tf_op jit(solution)/shard_map/reduce_scatter | solution.py:221
  (202 shorter events, 96.1 us)
Async XLA Ops:
  6.5 337.7 %copy-start = (bf16[1,360,2304]{2,1,0:T(8,128)(2,1)S(1)}, bf16[1,360,2304]{2,1,0:T(8,128)(2,1)}, u32[]{:S(2)}) copy-start(bf16[1,360,2304]{2,1,0:T(8,128)(2,1)} %param.39) | copy-start | bytes 4976644
  6.5 129.9 %all-gather.2.cloned.1.call-start = ((), (), s32[]{:S(2)}) async-start(), calls=%async_computation.7 | async-start | bytes 4456448 | tf_op jit(solution)/shard_map/all_gather | solution.py:91
  9.6 24.9 %all-to-all-start.1 = ((bf16[16,2,32]{2,1,0:T(2,128)(2,1)}), bf16[16,2,32]{2,1,0:T(2,128)(2,1)S(1)}, u32[]{:S(2)}, u32[]{:S(2)}) async-start(bf16[16,2,32]{2,1,0:T(2,128)(2,1)} %broadcast_in_dim.168), calls=%async_computation.1 | async-start | bytes 16384 | tf_op jit(solution)/shard_map/all_to_all | solution.py:153
  19.4 5.4 %copy-start.36 = (f32[256]{0:T(256)}, f32[256]{0:T(256)S(1)}, u32[]{:S(2)}) copy-start(f32[256]{0:T(256)S(1)} %add_rsqrt_fusion.1) | copy-start | bytes 3076
  26.9 4.9 copy-start.8
  34.5 22.1 %all-to-all-start = ((bf16[16,2,32,256]{3,2,1,0:T(8,128)(2,1)}), bf16[16,2,32,256]{3,2,1,0:T(8,128)(2,1)}, u32[]{:S(2)}, u32[]{:S(2)}) async-start(bf16[16,2,32,256]{3,2,1,0:T(8,128)(2,1)} %pad_maximum_fusion.1), calls=%async_computation | async-start | bytes 1048576 | tf_op jit(solution)/shard_map/all_to_all | solution.py:152
  78.7 5.4 %copy-start.16 = (bf16[1,1,1024,256]{2,3,1,0:T(8,128)(2,1)S(1)}, bf16[1,1,1024,256]{2,3,1,0:T(8,128)(2,1)}, u32[]{:S(2)}) copy-start(bf16[1,1,1024,256]{2,3,1,0:T(8,128)(2,1)} %copy.270) | copy-start | bytes 1572868
  88.7 11.7 %copy-start.9 = (f32[16,1,32,256]{3,2,0,1:T(8,128)S(1)}, f32[16,1,32,256]{3,2,0,1:T(8,128)}, u32[]{:S(2)}) copy-start(f32[16,1,32,256]{3,2,0,1:T(8,128)} %stack_reshape.25) | copy-start | bytes 1572868
  93.0 19.3 %copy-start.26 = (f32[8,32,4]{1,2,0:T(4,128)S(1)}, f32[8,32,4]{1,2,0:T(4,128)}, u32[]{:S(2)}) copy-start(f32[8,32,4]{1,2,0:T(4,128)} %copy-done.25) | copy-start | bytes 12292
  93.0 19.3 %copy-start.27 = (f32[8,32,4]{1,2,0:T(4,128)S(1)}, f32[8,32,4]{1,2,0:T(4,128)}, u32[]{:S(2)}) copy-start(f32[8,32,4]{1,2,0:T(4,128)} %fusion.78) | copy-start | bytes 12292
  93.0 20.7 %copy-start.37 = (f32[256]{0:T(256)S(1)}, f32[256]{0:T(256)}, u32[]{:S(2)}) copy-start(f32[256]{0:T(256)} %copy-done.36) | copy-start | bytes 3076
  93.0 14.9 %all-to-all-start.2 = ((f32[16,1,256]{2,1,0:T(1,128)}), f32[16,1,256]{2,1,0:T(1,128)S(1)}, u32[]{:S(2)}, u32[]{:S(2)}) async-start(f32[16,1,256]{2,1,0:T(1,128)} %reshape.488), calls=%async_computation.2 | async-start | bytes 32768 | tf_op jit(solution)/shard_map/all_to_all | solution.py:170
  107.9 19.3 %all-to-all-start.3 = ((f32[16,2,32,256]{3,2,1,0:T(8,128)}), f32[16,2,32,256]{3,2,1,0:T(8,128)}, u32[]{:S(2)}, u32[]{:S(2)}) async-start(f32[16,2,32,256]{3,2,1,0:T(8,128)} %pad_maximum_fusion), calls=%async_computation.3 | async-start | bytes 2097152 | tf_op jit(solution)/shard_map/all_to_all | solution.py:169
  112.3 5.7 %copy-start.15 = (f32[8,32,4,32]{1,3,2,0:T(8,128)S(1)}, f32[8,32,4,32]{1,3,2,0:T(8,128)}, u32[]{:S(2)}) copy-start(f32[8,32,4,32]{1,3,2,0:T(8,128)} %copy-done.14) | copy-start | bytes 393220
  112.3 133.5 %all-reduce.5.cloned.1.call-start = ((), (), s32[]{:S(2)}) async-start(), calls=%async_computation.8 | async-start | bytes 4718592 | tf_op jit(solution)/shard_map/psum | solution.py:185
  167.5 10.2 %copy-start.32 = (f32[256,4]{0,1:T(4,128)S(1)}, f32[256,4]{0,1:T(4,128)}, u32[]{:S(2)}) copy-start(f32[256,4]{0,1:T(4,128)} %add.217) | copy-start | bytes 12292
  167.5 10.2 %copy-start.31 = (f32[1,256,4]{1,2,0:T(4,128)S(1)}, f32[1,256,4]{1,2,0:T(4,128)}, u32[]{:S(2)}) copy-start(f32[1,256,4]{1,2,0:T(4,128)} %add.216) | copy-start | bytes 12292
  167.6 10.3 %copy-start.12 = (f32[1,256,4,64]{1,3,2,0:T(8,128)S(1)}, f32[1,256,4,64]{1,3,2,0:T(8,128)}, u32[]{:S(2)}) copy-start(f32[1,256,4,64]{1,3,2,0:T(8,128)} %copy.282) | copy-start | bytes 786436
  167.6 10.3 %copy-start.13 = (f32[1,256,4,64]{1,3,2,0:T(8,128)S(1)}, f32[1,256,4,64]{1,3,2,0:T(8,128)}, u32[]{:S(2)}) copy-start(f32[1,256,4,64]{1,3,2,0:T(8,128)} %copy.281) | copy-start | bytes 786436
  181.1 276.2 %reduce-scatter.3.cloned.1.call-start = ((), (), s32[]{:S(2)}) async-start(), calls=%async_computation.9 | async-start | bytes 15040512 | tf_op jit(solution)/shard_map/reduce_scatter | solution.py:218
  181.8 67.5 %copy-start.29 = (f32[2304]{0:T(1024)S(1)}, f32[2304]{0:T(1024)}, u32[]{:S(2)}) copy-start(f32[2304]{0:T(1024)} %param.34) | copy-start | bytes 27652
  250.5 89.6 %copy-start.39 = (bf16[1,2304,360]{1,2,0:T(8,128)(2,1)S(1)}, bf16[1,2304,360]{1,2,0:T(8,128)(2,1)}, u32[]{:S(2)}) copy-start(bf16[1,2304,360]{1,2,0:T(8,128)(2,1)} %param.37) | copy-start | bytes 4976644
  358.6 135.6 %reduce-scatter.5.cloned.1.call-start = ((), (), s32[]{:S(2)}) async-start(), calls=%async_computation.10 | async-start | bytes 2654208 | tf_op jit(solution)/shard_map/reduce_scatter | solution.py:221
  457.3 38.6 %copy-start.1 = (bf16[1,360,2304]{2,1,0:T(8,128)(2,1)S(1)}, bf16[1,360,2304]{2,1,0:T(8,128)(2,1)}, u32[]{:S(2)}) copy-start(bf16[1,360,2304]{2,1,0:T(8,128)(2,1)} %param.39) | copy-start | bytes 4976644
  (25 other events, 64.2 us)
Sparse Core Ops, SparseCore 0:
  9.6 59.0 all-gather.1
  181.2 64.4 all-reduce.4
  358.7 98.5 reduce-scatter.2
  461.3 32.7 reduce-scatter.4
